TPU v7x, 32 devices: a whole 2x2x4 slice. The times are simulated.
32 devices in a mesh: groups: 2 (over y), vox: 4 (over z), freq: 2 (over x), sub: 2 (over core).
Axes of the slice: x: 2, y: 2, z: 4, core: 2. Of those that a mesh axis runs over, the one named last changes fastest.
Arguments:
- residual: bfloat16 [4, 1024, 1024], P(('groups', 'freq'), 'vox', 'sub'), parts along dimension 0, may hold values from -6 to 6
- green: bfloat16 [4, 1024, 8192], P(('groups', 'freq'), None, 'vox'), parts along dimension 0, may hold values from -0.15625 to 0.15625
- active: int32 [4, 1024], P(('groups', 'freq')), parts along dimension 0, may hold values 0 or 1
- aperture: int32 [4], P(('groups', 'freq')), parts along dimension 0, may hold values from 256 to 511
- step_gain: float32 [4], P(('groups', 'freq')), parts along dimension 0, may hold values from 6 to 24
- block_region: int32 [128], P(('groups', 'vox')), parts along dimension 0, may hold values from 0 to 15
- strength: float32 [16], replicated, may hold values from 0.1 to 1
Outputs:
- updated: float32 [4, 1024, 1024], P(('groups', 'freq'), 'vox', 'sub'), parts along dimension 0
There are 2 independent parts, one for each index of `groups`. A program takes and returns all parts, laid end to end along the dimension named above; an argument that names none is the same for every part. Nothing has to cross between parts.
All inputs are finite; a program needn't handle non-finite values. No bound on the sum of `active` on one device may be relied on, other than what follows from the above.
Results may differ from a plain program's by a relative error of at most 0.0026.
Values may be sent and summed in bfloat16 or wider, within the bound.
A program may use at most 64 MiB of HBM per device.

v0:
```python
import jax
import jax.numpy as jnp
from jax import lax
from jax.experimental import pallas as pl
from jax.experimental.pallas import tpu as pltpu
from jax.sharding import PartitionSpec as P

BLOCK = 128
LANES = 128
APERTURE_MAX = 511
smooth_sq = 0.0625
FULL, UP, DOWN = range(3)
MESH = pl.DeviceIdType.MESH


def penalize(image_sum, strength_map):
    return image_sum - strength_map * image_sum / jnp.sqrt(image_sum * image_sum + smooth_sq)


def make_kernel(n, nf, ns, rows, cols, ne, vox_local, n_blocks, regions):
    tile = min(rows, LANES)
    per = rows // tile
    col_tiles = cols // LANES
    vchunk = min(512, vox_local)
    peers = nf * ns

    def kernel(
        res, green, active_in, aperture_in, gain_in, region_in, strength_in, out,
        active, aperture, gain, region, strength, sem_small,
        allm, gv, act_col, mm, img, ar_send, ar_land, wgt, gacc, flipped, send_buf, land_r, land_l,
        sem_g, sem_own, agr_s, agr_r, agl_s, agl_r, ar_s, ar_r, rsr_s, rsr_r, rsl_s, rsl_r,
    ):
        z = lax.axis_index("vox")
        f = lax.axis_index("freq")
        s = lax.axis_index("sub")
        has_up = z < n - 1
        has_down = z > 0
        up = {"vox": jnp.minimum(z + 1, n - 1)}
        down = {"vox": jnp.maximum(z - 1, 0)}

        def row_of(block):
            return pl.multiple_of(block * rows, rows)

        small = [
            pltpu.make_async_copy(a, b, sem_small.at[i])
            for i, (a, b) in enumerate((
                (active_in, active), (aperture_in, aperture), (gain_in, gain),
                (region_in, region), (strength_in, strength),
            ))
        ]
        for c in small:
            c.start()
        own_copy = pltpu.make_async_copy(res, allm.at[pl.ds(row_of(z), rows), :], sem_own)
        own_copy.start()
        green_copy = pltpu.make_async_copy(green, gv, sem_g)
        green_copy.start()

        def peer(k):
            df, ds = k // ns, k % ns
            return {"freq": lax.rem(f + df, nf), "sub": lax.rem(s + ds, ns)}

        barrier = pltpu.get_barrier_semaphore()
        for k in range(1, peers):
            pl.semaphore_signal(barrier, inc=1, device_id=peer(k), device_id_type=MESH)

        @pl.when(has_up)
        def _():
            pl.semaphore_signal(barrier, inc=1, device_id=up, device_id_type=MESH)

        @pl.when(has_down)
        def _():
            pl.semaphore_signal(barrier, inc=1, device_id=down, device_id_type=MESH)

        pl.semaphore_wait(barrier, peers - 1 + has_up.astype(jnp.int32) + has_down.astype(jnp.int32))

        def square(q):
            local = q * tile - s * cols
            inside = (local >= 0) & (local < cols)
            return inside, lax.div(jnp.clip(local, 0, cols - 1), LANES)

        def band(q, kind):
            reach = q * tile - s * cols + ne
            shift = ne // LANES + APERTURE_MAX // LANES + 1
            lift = LANES * (shift - ne // LANES)
            first = lax.div(reach + lift - APERTURE_MAX, LANES) - shift
            last = lax.div(reach + lift + tile - 1 + APERTURE_MAX, LANES) - shift + 1
            first = jnp.clip(first, 0, col_tiles)
            last = jnp.clip(last, 0, col_tiles)
            if kind != FULL:
                inside, diag = square(q)
            if kind == UP:
                last = jnp.where(inside, jnp.minimum(last, diag + 1), last)
            if kind == DOWN:
                first = jnp.where(inside, jnp.maximum(first, diag), first)
            return first, last - first

        def per_width(q, fn, kind=FULL):
            first, count = band(q, kind)
            for w in range(1, col_tiles + 1):
                @pl.when(count == w)
                def _(w=w):
                    fn(pl.ds(pl.multiple_of(first * LANES, LANES), w * LANES))

        def tile_rows(q):
            return pl.ds(pl.multiple_of(q * tile, tile), tile)

        def remote(src, dst, send, recv, target):
            return pltpu.make_async_remote_copy(
                src_ref=src, dst_ref=dst, send_sem=send, recv_sem=recv,
                device_id=target, device_id_type=MESH,
            )

        def each_tile(block, make, act, kind=FULL):
            for t in range(per):
                q = block * per + t
                per_width(q, lambda c, q=q: act(make(q, c)), kind)

        def gather_up(q, c):
            a = allm.at[tile_rows(q), c]
            return remote(a, a, agr_s.at[q], agr_r.at[q], up)

        def gather_down(q, c):
            a = allm.at[tile_rows(q), c]
            return remote(a, a, agl_s.at[q], agl_r.at[q], down)

        for t in range(per):
            q = z * per + t

            def first_up(c, q=q, t=t):
                remote(res.at[pl.ds(t * tile, tile), c], allm.at[tile_rows(q), c],
                       agr_s.at[q], agr_r.at[q], up).start()

            def first_down(c, q=q, t=t):
                remote(res.at[pl.ds(t * tile, tile), c], allm.at[tile_rows(q), c],
                       agl_s.at[q], agl_r.at[q], down).start()

            @pl.when(has_up)
            def _():
                per_width(q, first_up)

            @pl.when(has_down)
            def _():
                per_width(q, first_down)

        for c in small:
            c.wait()
        for i in range(ne // LANES):
            line = active[0:1, i * LANES:(i + 1) * LANES].astype(jnp.float32)
            act_col[i * LANES:(i + 1) * LANES, :] = jnp.broadcast_to(line, (LANES, LANES)).T
        img[...] = jnp.zeros_like(img)
        col0 = pl.multiple_of(s * cols, cols)

        def pair_mask(block):
            r0 = row_of(block)
            rr = lax.broadcasted_iota(jnp.int32, (rows, cols), 0) + r0
            cc = lax.broadcasted_iota(jnp.int32, (rows, cols), 1) + col0
            in_band = jnp.abs(rr - cc) <= aperture[0]
            row_on = act_col[pl.ds(r0, rows), 0:1] > 0.5
            col_on = active[0:1, pl.ds(col0, cols)] > 0
            return in_band & row_on & col_on

        def image_part(block):
            r0 = row_of(block)
            value = allm[pl.ds(r0, rows), :].astype(jnp.float32)
            mm[...] = jnp.where(pair_mask(block), value, 0.0).astype(jnp.bfloat16)

            @pl.loop(0, vox_local // vchunk)
            def _(v):
                vs = pl.ds(pl.multiple_of(v * vchunk, vchunk), vchunk)
                y = jnp.dot(mm[...], gv[pl.ds(col0, cols), vs], preferred_element_type=jnp.float32)
                y = y * gv[pl.ds(r0, rows), vs].astype(jnp.float32)
                img[:, vs] += jnp.sum(y.reshape(rows // 8, 8, vchunk), axis=0)

        own_copy.wait()
        green_copy.wait()
        image_part(z)

        @pl.loop(0, n - 1)
        def _(step):
            from_below = z - 1 - step
            from_above = z + 1 + step
            for t in range(per):
                @pl.when(from_below >= 0)
                def _():
                    q = from_below * per + t

                    def land(c):
                        gather_up(q, c).wait_recv()

                        @pl.when(has_up)
                        def _():
                            gather_up(q, c).start()
                    per_width(q, land)

                @pl.when(from_above < n)
                def _():
                    q = from_above * per + t

                    def land(c):
                        gather_down(q, c).wait_recv()

                        @pl.when(has_down)
                        def _():
                            gather_down(q, c).start()
                    per_width(q, land)

            @pl.when(from_below >= 0)
            def _():
                image_part(from_below)

            @pl.when(from_above < n)
            def _():
                image_part(from_above)

        ar_send[...] = jnp.sum(img[...], axis=0, keepdims=True)
        exchanges = [
            remote(ar_send, ar_land.at[k], ar_s.at[k], ar_r.at[k], peer(k)) for k in range(1, peers)
        ]
        for e in exchanges:
            e.start()
        strength_map = jnp.concatenate(
            [jnp.full((1, BLOCK), strength[region[b]], jnp.float32) for b in range(n_blocks)], axis=1
        )

        @pl.loop(0, n)
        def _(b):
            @pl.when(has_up & (b <= z))
            def _():
                each_tile(b, gather_up, lambda c: c.wait_send())

            @pl.when(has_down & (b >= z))
            def _():
                each_tile(b, gather_down, lambda c: c.wait_send())

        for e in exchanges:
            e.wait_recv()
        total = ar_send[...]
        for k in range(1, peers):
            total = total + ar_land[k]
        img[0:1, :] = penalize(total, strength_map)

        wrows = 32

        @pl.loop(0, cols // wrows)
        def _(i):
            src = pl.ds(pl.multiple_of(col0 + i * wrows, wrows), wrows)
            dst = pl.ds(pl.multiple_of(i * wrows, wrows), wrows)
            wgt[dst, :] = (gv[src, :].astype(jnp.float32) * img[0:1, :]).astype(jnp.bfloat16)

        def scatter_up(q, c):
            return remote(send_buf.at[tile_rows(q), c], land_r.at[tile_rows(q), c],
                          rsr_s.at[q], rsr_r.at[q], up)

        def scatter_down(q, c):
            return remote(send_buf.at[tile_rows(q), c], land_l.at[tile_rows(q), c],
                          rsl_s.at[q], rsl_r.at[q], down)

        def partial_step(k, ends):
            lo, hi = ends
            use_hi = (hi > z) & ((lo >= z) | (z + (n - 1 - hi) <= (n - 1 - z) + lo))
            d = jnp.where(use_hi, hi, lo)
            rs = pl.ds(row_of(d), rows)
            part = lax.dot_general(
                gv[rs, :], wgt[...], (((1,), (1,)), ((), ())), preferred_element_type=jnp.float32
            )
            gacc[rs, :] = part
            sends_up = (d > z) & jnp.logical_not(has_down)
            sends_down = (d < z) & jnp.logical_not(has_up)

            @pl.when(sends_up | sends_down)
            def _():
                send_buf[rs, :] = part.astype(jnp.bfloat16)

            @pl.when(sends_up)
            def _():
                each_tile(d, scatter_up, lambda c: c.start(), UP)

            @pl.when(sends_down)
            def _():
                each_tile(d, scatter_down, lambda c: c.start(), DOWN)

            step_hi = use_hi.astype(jnp.int32)
            return lo + 1 - step_hi, hi - step_hi

        lax.fori_loop(0, n, partial_step, (jnp.int32(0), jnp.int32(n - 1)))

        @pl.loop(0, n - 1)
        def _(slot):
            @pl.when(has_down & (slot >= z))
            def _():
                d = z + n - 1 - slot
                for t in range(per):
                    q = d * per + t

                    def add(c):
                        scatter_up(q, c).wait_recv()
                        send_buf[tile_rows(q), c] = (
                            gacc[tile_rows(q), c] + land_r[tile_rows(q), c].astype(jnp.float32)
                        ).astype(jnp.bfloat16)
                        scatter_up(q, c).start()
                    per_width(q, add, UP)

            @pl.when(has_up & (slot >= n - 1 - z))
            def _():
                d = slot - (n - 1 - z)
                for t in range(per):
                    q = d * per + t

                    def add(c):
                        scatter_down(q, c).wait_recv()
                        send_buf[tile_rows(q), c] = (
                            gacc[tile_rows(q), c] + land_l[tile_rows(q), c].astype(jnp.float32)
                        ).astype(jnp.bfloat16)
                        scatter_down(q, c).start()
                    per_width(q, add, DOWN)

        @pl.when(has_down)
        def _():
            each_tile(z, scatter_up, lambda c: c.wait_recv(), UP)

        @pl.when(has_up)
        def _():
            each_tile(z, scatter_down, lambda c: c.wait_recv(), DOWN)

        mine = pl.ds(row_of(z), rows)
        def add_landed(land, there, q, mirrored):
            inside, diag = square(q)
            offset = lax.rem(q * tile, LANES)
            for j in range(col_tiles):
                c = slice(j * LANES, (j + 1) * LANES)
                flip = inside & mirrored(j, diag)

                @pl.when(there & jnp.logical_not(flip))
                def _():
                    gacc[tile_rows(q), c] += land[tile_rows(q), c].astype(jnp.float32)

                @pl.when(there & flip)
                def _():
                    twin = pl.ds(pl.multiple_of(col0 + j * LANES, LANES), LANES)
                    own = pl.ds(pl.multiple_of(diag * LANES, LANES), LANES)
                    flipped[...] = land[twin, own].astype(jnp.float32).T
                    gacc[tile_rows(q), c] += flipped[pl.ds(pl.multiple_of(offset, tile), tile), :]

        for t in range(per):
            add_landed(land_r, has_down, z * per + t, lambda j, diag: j > diag)
            add_landed(land_l, has_up, z * per + t, lambda j, diag: j < diag)
        gradient = gacc[mine, :]
        data = allm[mine, :].astype(jnp.float32)
        out[...] = jnp.where(pair_mask(z), data - gain[0] * gradient, 0.0)

        for e in exchanges:
            e.wait_send()

        @pl.loop(0, n)
        def _(b):
            @pl.when(has_up & (b > z))
            def _():
                each_tile(b, scatter_up, lambda c: c.wait_send(), UP)

            @pl.when(has_down & (b < z))
            def _():
                each_tile(b, scatter_down, lambda c: c.wait_send(), DOWN)

    tiles = n * per
    dma = pltpu.SemaphoreType.DMA
    scratch = [
        pltpu.VMEM((1, ne), jnp.int32),
        pltpu.SMEM((1,), jnp.int32),
        pltpu.SMEM((1,), jnp.float32),
        pltpu.SMEM((n_blocks,), jnp.int32),
        pltpu.SMEM((regions,), jnp.float32),
        dma((5,)),
        pltpu.VMEM((ne, cols), jnp.bfloat16),
        pltpu.VMEM((ne, vox_local), jnp.bfloat16),
        pltpu.VMEM((ne, LANES), jnp.float32),
        pltpu.VMEM((rows, cols), jnp.bfloat16),
        pltpu.VMEM((8, vox_local), jnp.float32),
        pltpu.VMEM((1, vox_local), jnp.float32),
        pltpu.VMEM((peers, 1, vox_local), jnp.float32),
        pltpu.VMEM((cols, vox_local), jnp.bfloat16),
        pltpu.VMEM((ne, cols), jnp.float32),
        pltpu.VMEM((LANES, LANES), jnp.float32),
        pltpu.VMEM((ne, cols), jnp.bfloat16),
        pltpu.VMEM((ne, cols), jnp.bfloat16),
        pltpu.VMEM((ne, cols), jnp.bfloat16),
        dma, dma,
        dma((tiles,)), dma((tiles,)), dma((tiles,)), dma((tiles,)),
        dma((peers,)), dma((peers,)),
        dma((tiles,)), dma((tiles,)), dma((tiles,)), dma((tiles,)),
    ]
    return kernel, scratch


def solution(mesh):
    sizes = dict(mesh.shape)

    def body(residual, green, active, aperture, step_gain, block_region, strength):
        _, rows, cols = residual.shape
        _, ne, vox_local = green.shape
        kernel, scratch = make_kernel(
            sizes["vox"], sizes["freq"], sizes["sub"], rows, cols, ne, vox_local,
            block_region.shape[0], strength.shape[0],
        )
        vmem = pl.BlockSpec(memory_space=pltpu.VMEM)
        hbm = pl.BlockSpec(memory_space=pltpu.HBM)
        updated = pl.pallas_call(
            kernel,
            out_shape=jax.ShapeDtypeStruct((rows, cols), jnp.float32),
            in_specs=[hbm] * 7,
            out_specs=vmem,
            scratch_shapes=scratch,
            compiler_params=pltpu.CompilerParams(
                collective_id=0, has_side_effects=True, vmem_limit_bytes=60 * 1024 * 1024
            ),
            name="imaging_step",
        )(residual[0], green[0], active, aperture, step_gain, block_region, strength)
        return updated[None]

    in_specs = (
        P(("groups", "freq"), "vox", "sub"),
        P(("groups", "freq"), None, "vox"),
        P(("groups", "freq"), None),
        P(("groups", "freq")),
        P(("groups", "freq")),
        P(("groups", "vox")),
        P(),
    )
    out_specs = P(("groups", "freq"), "vox", "sub")
    return jax.shard_map(body, mesh=mesh, in_specs=in_specs, out_specs=out_specs, check_vma=False)
```

profile of v0, /device:TPU:0, one launch (start us, length us, event | category | flops | bytes accessed | tf_op | source)
XLA Modules:
  0.0 46.5 jit_solution(18380856327958170035)
XLA Ops:
  1.3 43.3 %imaging_step.1 = f32[256,512]{1,0:T(8,128)} custom-call(bf16[256,512]{1,0:T(8,128)(2,1)} %bitcast.5, bf16[1024,2048]{1,0:T(8,128)(2,1)} %bitcast.3, s32[1,1024]{1,0:T(1,128)} %active_in.1, s32[1]{0:T(128)S(6)} %copy.9.aperture_in, f32[1]{0:T(128)S(6)} %copy.10.gain_in, s32[16]{0:T(128)} %region_in.1, f32[16]{0:T(128)} %strength_in.1), custom_call_target="tpu_custom_call" | custom-call | tf_op jit(solution)/shard_map/imaging_step/pallas_call | solution.py:406
  44.6 1.9 %copy.11 = f32[1,256,512]{2,1,0:T(8,128)} copy(f32[1,256,512]{2,1,0:T(8,128)} %bitcast.4) | data formatting | bytes 1048576
where the time goes:
time: 46.7 us; the launch traced here: 46.5 us
  Pallas kernels  43.3 us (93%)
  local copies, waits for them, and re-layouts  1.87 us (4%)
  between operations  1.3 us (3%)
    pallas_call x1, Pallas kernels, body(): pl.pallas_call(kernel, out_shape=jax.ShapeDtypeStruct((rows, cols), jnp.f...  43.3 us
    unnamed x1, local copies, waits for them, and re-layouts  1.87 us

commit v1 on v0

--- a/solution.py
+++ b/solution.py
@@ -410,10 +410,13 @@
             out_specs=vmem,
             scratch_shapes=scratch,
             compiler_params=pltpu.CompilerParams(
-                collective_id=0, has_side_effects=True, vmem_limit_bytes=60 * 1024 * 1024
+                collective_id=0, has_side_effects=True, vmem_limit_bytes=24 * 1024 * 1024
             ),
             name="imaging_step",
-        )(residual[0], green[0], active, aperture, step_gain, block_region, strength)
+        )(*[
+            pltpu.with_memory_space_constraint(a, pltpu.HBM) if a.size > 1 else a
+            for a in (residual[0], green[0], active, aperture, step_gain, block_region, strength)
+        ])
         return updated[None]
 
     in_specs = (

time: 46.7 us -> 44.8 us (0.959)
  local copies, waits for them, and re-layouts: 1.87 us -> 0.8 us
  Pallas kernels: 43.3 us -> 42.5 us
    unnamed x1, local copies, waits for them, and re-layouts: 1.87 us -> 0.8 us
    pallas_call x1, Pallas kernels: 43.3 us -> 42.5 us  [body(): pl.pallas_call(kernel, out_shape=jax.ShapeDtypeStruct((rows, cols), jnp.f...]
where the time goes in v1:
time: 44.8 us; the launch traced here: 44.6 us
  Pallas kernels  42.5 us (95%)
  between operations  1.3 us (3%)
  local copies, waits for them, and re-layouts  0.8 us (2%)
    pallas_call x1, Pallas kernels, body(): pl.pallas_call(kernel, out_shape=jax.ShapeDtypeStruct((rows, cols), jnp.f...  42.5 us

profile of v1, /device:TPU:0, one launch (start us, length us, event | category | flops | bytes accessed | tf_op | source)
XLA Modules:
  0.0 44.6 jit_solution(6558972332795177311)
XLA Ops:
  1.3 42.5 %imaging_step.1 = f32[256,512]{1,0:T(8,128)S(1)} custom-call(bf16[256,512]{1,0:T(8,128)(2,1)} %bitcast.5, bf16[1024,2048]{1,0:T(8,128)(2,1)} %bitcast.4, s32[1,1024]{1,0:T(1,128)} %active_in.1, s32[1]{0:T(128)S(6)} %copy.9.aperture_in, f32[1]{0:T(128)S(6)} %copy.10.gain_in, s32[16]{0:T(128)} %region_in.1, f32[16]{0:T(128)} %strength_in.1), custom_call_target="tpu_custom_call" | custom-call | tf_op jit(solution)/shard_map/imaging_step/pallas_call | solution.py:406
  43.8 0.8 %copy.11 = f32[1,256,512]{2,1,0:T(8,128)} copy(f32[1,256,512]{2,1,0:T(8,128)S(1)} %bitcast.3) | data formatting | bytes 1048576

commit v2 on v1

--- a/solution.py
+++ b/solution.py
@@ -1,3 +1,6 @@
+import heapq
+import itertools
+
 import jax
 import jax.numpy as jnp
 from jax import lax
@@ -11,10 +14,838 @@
 smooth_sq = 0.0625
 FULL, UP, DOWN = range(3)
 MESH = pl.DeviceIdType.MESH
+REACH = (APERTURE_MAX + LANES - 1) // LANES
+CHUNK = 512
+LN2 = 0.6931471805599453
+STEPS = 32600.0
 
 
 def penalize(image_sum, strength_map):
     return image_sum - strength_map * image_sum / jnp.sqrt(image_sum * image_sum + smooth_sq)
+
+
+WIRE, HOP_FIRST, HOP = 0.354, 2.3, 2.0
+IMAGE, PLACE, MERGE, PARTIAL, WEIGHT, ADD = 0.47, 0.04, 0.1, 0.47, 0.2, 0.12
+EXCHANGE, LAG, PATIENCE, SLACK, ACROSS = 2.8, 0.0, 1.0, 0.8, 1.0
+
+
+def tile_pairs(tiles, reach):
+    return [(p, q) for p in range(tiles) for q in range(p, min(tiles, p + reach + 1))]
+
+
+def riders(pairs, n, per, half, cores):
+    if cores != 2 or half != REACH or REACH % per or REACH * LANES <= APERTURE_MAX:
+        return {}
+    index = {pair: a for a, pair in enumerate(pairs)}
+    return {a: (index[p, p], index[q, q]) for a, (p, q) in enumerate(pairs) if q - p == REACH}
+
+
+def lanes_of(pairs, n, per, half, cores, ride):
+    sizes = {}
+    for p, q in pairs:
+        sizes[p // per, q // per] = sizes.get((p // per, q // per), 0) + 1
+    lanes = {}
+    for k in range(n):
+        load, follows, light = [0] * cores, {}, {}
+        for a in ride:
+            i, j = pairs[a][0] // per, pairs[a][1] // per
+            for own, there in ((i, k > i), (j, k < j)):
+                if there:
+                    follows[own, own] = i, j
+                    light[own, own] = light.get((own, own), 0) + 1
+
+        def rank(block, k=k):
+            i, j = block
+            far = n - 1 - j if k == 0 else i if k == n - 1 else k not in block
+            return far, k not in block, -sizes[block], block
+
+        def weight(block, k=k, light=light):
+            return (sizes[block] - light.get(block, 0)) * (block != (k, k) or 0 < k < n - 1)
+
+        order = sorted(sizes, key=rank)
+        forced = {(i, j): (j if k == i else i) * per // half for i, j in order if k in (i, j)}
+        free = [block for block in order if block not in forced and block not in follows]
+
+        def filled(where, follows=follows, forced=forced):
+            return {**{block: where[to] for block, to in follows.items() if block not in forced}, **where}
+
+        def unevenness(picks):
+            where = filled({**forced, **dict(zip(free, picks))})
+            total, worst = [0] * cores, []
+            for at, block in enumerate(order):
+                total[where[block]] += weight(block)
+                if at + 1 == len(order) or rank(order[at + 1])[0] != rank(block)[0]:
+                    worst.append(max(total) - min(total))
+            return sum(worst), picks
+
+        if cores ** len(free) <= 4096:
+            chosen = dict(zip(free, min(map(unevenness, itertools.product(range(cores), repeat=len(free))))[1]))
+        else:
+            chosen = {}
+            for block in free:
+                chosen[block] = load.index(min(load))
+                load[chosen[block]] += weight(block)
+        chosen = filled({**forced, **chosen})
+        for a, (p, q) in enumerate(pairs):
+            lanes[a, k] = chosen[p // per, q // per]
+    return lanes
+
+
+def colours(uses):
+    taken, chosen = {}, {}
+    for a in sorted(uses, key=lambda a: (-len(uses[a]), a)):
+        colour = 0
+        while any(colour in taken.setdefault(place, set()) for place in uses[a]):
+            colour += 1
+        for place in uses[a]:
+            taken[place].add(colour)
+        chosen[a] = colour
+    return chosen
+
+
+class Network:
+    def __init__(self, cores, hop):
+        self.cores, self.hop, self.queue, self.count = cores, hop, [], 0
+        self.wires = {}
+
+    def post(self, time, what):
+        self.count += 1
+        heapq.heappush(self.queue, (time, self.count, what))
+
+    def send(self, k, c, step, time, what):
+        lines, turn, free = self.wires.setdefault((k, step), ([[] for _ in range(self.cores)], 0, 0.0))
+        lines[c].append(what)
+        self.post(max(time, free), ("wire", k, step, 0, 0))
+
+    def serve(self, k, step, now):
+        lines, turn, free = self.wires[k, step]
+        if free > now + 1e-9:
+            return
+        for c in range(self.cores):
+            line = lines[(turn + c) % self.cores]
+            if line:
+                self.post(now + WIRE + self.hop, line.pop(0))
+                self.wires[k, step] = lines, (turn + c + 1) % self.cores, now + WIRE
+                self.post(now + WIRE, ("wire", k, step, 0, 0))
+                return
+
+
+def gather_plan(pairs, n, per, half, cores, lanes, ride):
+    net = Network(cores, HOP_FIRST)
+    own, events = {}, {}
+    seen, busy, missing = set(), {}, {}
+    low = {pair[0]: a for a, pair in ride.items()}
+    high = {pair[1]: a for a, pair in ride.items()}
+    for p, q in pairs:
+        for k in range(n):
+            missing[p // per, q // per, k] = missing.get((p // per, q // per, k), 0) + 1
+
+    def send(k, c, a, step, kind, now):
+        net.send(k, c, step, now, (kind, k + step, lanes[a, k + step], a, 0))
+
+    for k in range(n):
+        for c in range(cores):
+            own[k, c], events[k, c] = [], []
+        mine = []
+        for a, (p, q) in enumerate(pairs):
+            i, j = p // per, q // per
+            c = lanes[a, k]
+            if i == k < j:
+                mine.append((j - i, c, a, 0, q, 1, 0))
+            elif i < k == j:
+                mine.append((j - i, c, a, 1, p, 0, 1))
+            elif i == j == k:
+                mine.append((n, c, a, 0, q, int(p == q and a not in low), int(p == q and a not in high)))
+                if p < q:
+                    mine.append((n, c, a, 1, p, 0, 0))
+        for _, c, a, second, other, up, down in sorted(mine):
+            p, q = pairs[a]
+            up, down = up and k < n - 1 and a not in ride, down and k > 0 and a not in ride
+            side = a in low and k < n - 1 or a in high and k > 0
+            own[k, c].append((a, second, (q if second else p) % per, other % half, up, down, side))
+            if side:
+                net.post(0.1 + WIRE + ACROSS, ("lift", k, 1 - c, a, 0))
+            if up:
+                send(k, c, a, 1, "A", 0.1)
+            if down:
+                send(k, c, a, -1, "B" if second else "A", 0.1)
+        for c in range(cores):
+            here = [a for a, (p, q) in enumerate(pairs) if p // per == q // per == k and lanes[a, k] == c]
+            for a in sorted(here, key=lambda a: pairs[a][0] == pairs[a][1]):
+                net.post(0.5, ("own", k, c, a, 0))
+    while net.queue:
+        now, _, (kind, k, c, a, _) = heapq.heappop(net.queue)
+        if kind == "wire":
+            net.serve(k, c, now)
+            continue
+        at = busy.get((k, c), 0.0)
+        if at > now + 1e-9:
+            net.post(at, (kind, k, c, a, 0))
+            continue
+        p, q = pairs[a]
+        i, j = p // per, q // per
+        e = dict(a=a, wait=int(kind != "own"), second=int(kind == "B"), fup=0, fdn=0, merge=0, cup=0, cdn=0, comp=0, run=0)
+        e.update(blend=0, ride=0, lift=0, other=0, lower=0, rest=0)
+        if kind == "lift":
+            up = a in low
+            e.update(a=low[a] if up else high[a], second=int(not up), fup=int(up), fdn=int(not up))
+            e.update(lift=1, blend=1, other=a, lower=int(not up))
+            a = e["a"]
+        elif kind in ("rideA", "rideB"):
+            e.update(wait=0, ride=1, comp=1, lower=int(kind == "rideB"), other=low[a] if k > i else high[a])
+        elif kind == "own":
+            e["comp"] = 1
+            if p < q:
+                e.update(merge=1, cup=int(k < n - 1), cdn=int(k > 0))
+        elif j < k:
+            e.update(fup=int(k < n - 1), comp=1)
+        elif i > k:
+            e.update(fdn=int(k > 0), comp=1)
+        else:
+            if kind == "A":
+                e["fup"] = int(k < j)
+            else:
+                e["fdn"] = int(k > i)
+            whole = k in (i, j) or (a, k) in seen
+            seen.add((a, k))
+            if whole:
+                e.update(merge=1, comp=1, cup=int(k == j and k < n - 1), cdn=int(k == i and k > 0))
+                e.update(blend=int(a in ride and k in (i, j)), lower=int(k == i))
+        if a in ride and kind in ("A", "B"):
+            if kind == "A" and k > i:
+                net.post(now, ("rideA", k, c, ride[a][0], 0))
+            if k < j and (kind == "B" or k < i):
+                net.post(now, ("rideB" if kind == "B" else "rideA", k, c, ride[a][1], 0))
+        for flag, step, sent in (("fup", 1, "A"), ("fdn", -1, "B" if e["second"] else "A"), ("cup", 1, "A"), ("cdn", -1, "A")):
+            if e[flag]:
+                send(k, c, a, step, sent, now + 0.05 + MERGE * e["merge"])
+        if e["comp"]:
+            block = pairs[a][0] // per, pairs[a][1] // per, k
+            missing[block] -= 1
+            e["run"] = int(missing[block] == 0)
+            e["rest"] = int(e["run"] and block[0] <= k <= block[1])
+        busy[k, c] = now + 0.06 + MERGE * (e["merge"] + e["ride"] + e["blend"] * (1 - e["merge"])) + PLACE * e["comp"] + IMAGE * e["run"]
+        events[k, c].append(e)
+    return own, events, [max(busy[k, c] for c in range(cores)) for k in range(n)]
+
+
+def scatter_plan(pairs, n, per, half, cores, lanes, ride, starts):
+    low = {pair[0]: a for a, pair in ride.items()}
+    high = {pair[1]: a for a, pair in ride.items()}
+
+    def ends(a):
+        return pairs[a][0] // per, pairs[a][1] // per
+
+    def run(order):
+        net = Network(cores, HOP)
+        events = {key: [] for key in order}
+        busy, got, weighted, ready = {}, {}, set(), set()
+        made = {key: 0 for key in order}
+        waiting = {key: [] for key in order}
+        for k, c in order:
+            busy[k, c] = starts[k]
+            net.post(starts[k], ("go", k, c, -1, 0))
+
+        def handle(k, c, a, kind, now):
+            i, j = ends(a)
+            e = dict(a=a, comp=int(kind == "D"), first=0, wait=int(kind in ("U", "V")), v=int(kind in ("V", "down")))
+            e.update(u=int(kind == "U"), up=0, dn=0, fini=0, finj=0, blend=0, side=0, other=0, mean=0, second=0)
+            cost = ADD
+            if kind == "D":
+                e["first"] = int((j, k, c) not in weighted)
+                weighted.add((j, k, c))
+                e["mean"] = int(made[k, c] > 1 or 0 < k < n - 1)
+                if e["mean"]:
+                    e["second"] = int((i, k, c) not in weighted)
+                    weighted.add((i, k, c))
+                cost = PARTIAL * (1 + e["mean"]) + WEIGHT * (e["first"] + e["second"]) + 0.06
+            elif not e["wait"]:
+                e["up"], e["dn"] = int(kind == "up"), int(kind == "down")
+            else:
+                got.setdefault((a, k), set()).add(kind)
+                e["up"], e["dn"] = int(kind == "U" and k < j), int(kind == "V" and k > i)
+                need = int(0 < k <= j) + int(i <= k < n - 1)
+                if k in (i, j) and len(got[a, k]) == need:
+                    e.update(fini=int(k == i), finj=int(k == j and pairs[a][0] < pairs[a][1]))
+            if a in ride:
+                e["blend"] = int(e["up"] or e["dn"])
+                if e["wait"] and k == (j if kind == "U" else i):
+                    d = ride[a][kind == "U"]
+                    e.update(side=1, other=d)
+                    cost += 0.1
+                    net.post(now + cost + WIRE + ACROSS, (kind, k, 1 - c, d, 0))
+            done = now + cost
+            cost += 0.1 * (e["fini"] or e["finj"])
+            if e["up"]:
+                net.send(k, c, 1, done, ("U", k + 1, lanes[a, k + 1], a, 0))
+            if e["dn"]:
+                net.send(k, c, -1, done, ("V", k - 1, lanes[a, k - 1], a, 0))
+            events[k, c].append(e)
+            now += cost
+            if kind == "D":
+                for x in sorted(range(len(pairs)), key=lambda x: (x not in ride, x)):
+                    if ends(x) == (i, j):
+                        ready.add((x, k))
+                        if k == 0 < j and x not in high:
+                            now = handle(k, c, x, "up", now)
+                        if k == n - 1 > i and x not in low:
+                            now = handle(k, c, x, "down", now)
+            busy[k, c] = now
+            return now
+
+        while net.queue:
+            now, _, (kind, k, c, a, _) = heapq.heappop(net.queue)
+            if kind == "wire":
+                net.serve(k, c, now)
+                continue
+            if kind != "go":
+                i, j = ends(a)
+                last = k == (j if kind == "U" else i) and a not in ride
+                waiting[k, c].append((now + PATIENCE * last, a, kind))
+            if busy[k, c] > now + 1e-9:
+                continue
+            todo = order[k, c]
+            more = made[k, c] < len(todo)
+            hit = min((
+                w for w in waiting[k, c]
+                if (w[1], k) in ready and all((d, k) in ready or lanes[d, k] != c for d in ride.get(w[1], ()))
+            ), default=None)
+            if hit is not None and hit[0] + SLACK * more <= now + 1e-9:
+                waiting[k, c].remove(hit)
+                net.post(handle(k, c, hit[1], hit[2], now), ("go", k, c, -1, 0))
+            elif more:
+                made[k, c] += 1
+                net.post(handle(k, c, todo[made[k, c] - 1], "D", now), ("go", k, c, -1, 0))
+            elif hit is not None:
+                net.post(hit[0], ("go", k, c, -1, 0))
+        return events, max(busy.values())
+
+    order = {}
+    for k in range(n):
+        for c in range(cores):
+            def rank(a, k=k):
+                i, j = ends(a)
+                return min(n - 1 - j + k, i + n - 1 - k), any(ends(x) == (i, j) for x in ride), a
+            first = [a for a in range(len(pairs)) if all(ends(x) != ends(a) for x in range(a))]
+            order[k, c] = sorted((a for a in first if lanes[a, k] == c), key=rank)
+    return run(order)
+
+
+def plans(n, per, half, cores):
+    pairs = tile_pairs(n * per, REACH)
+    count = len(pairs)
+    ride = riders(pairs, n, per, half, cores)
+    lanes = lanes_of(pairs, n, per, half, cores, ride)
+    own, gather, ends = gather_plan(pairs, n, per, half, cores, lanes, ride)
+    scatter, _ = scatter_plan(pairs, n, per, half, cores, lanes, ride, [
+        end + EXCHANGE + LAG * (k in (0, n - 1)) for k, end in enumerate(ends)
+    ])
+
+    def landings(plan, which):
+        uses = {}
+        for place, line in plan.items():
+            for e in line:
+                a = which(e)
+                if a is not None:
+                    uses.setdefault(a, set()).add(place)
+        chosen = colours(uses)
+        return chosen, max(chosen.values(), default=-1) + 1
+
+    first_a, size_a = landings(
+        gather, lambda e: e["other"] if e["lift"] else e["a"] if e["wait"] and not e["second"] else None
+    )
+    first_b, size_b = landings(gather, lambda e: e["a"] if e["wait"] and e["second"] and not e["lift"] else None)
+    first_u, size_u = landings(scatter, lambda e: e["a"] if e["wait"] and e["u"] else None)
+    first_v, size_v = landings(scatter, lambda e: e["a"] if e["wait"] and e["v"] else None)
+
+    def word(a, k, flags):
+        p, q = pairs[a]
+        code = a | p << 8 | q << 13
+        for bit, flag in enumerate(flags):
+            code |= int(flag) << (18 + bit)
+        if k < n - 1:
+            code |= lanes[a, k + 1] << 28
+        if k > 0:
+            code |= lanes[a, k - 1] << 29
+        return code
+
+    def ag_sem(a, twin):
+        return size_a + first_b.get(a, 0) if twin else first_a.get(a, 0)
+
+    def rs_sem(a, turned):
+        return size_u + first_v.get(a, 0) if turned else first_u.get(a, 0)
+
+    def gather_sems(e):
+        waits = ag_sem(e["other"], 0) if e["lift"] else ag_sem(e["a"], e["second"])
+        sends = ag_sem(e["a"], 0 if e["cup"] or e["cdn"] or e["fup"] else e["second"])
+        return waits | sends << 8 | e["other"] << 16 | e["lower"] << 24 | e["ride"] << 25 | e["lift"] << 26 | e["rest"] << 27
+
+    def scatter_sems(e):
+        turned = int(e["dn"] or not e["up"] and e["v"])
+        sends = rs_sem(e["other"] if e["side"] else e["a"], turned)
+        return rs_sem(e["a"], e["v"]) | sends << 8 | e["other"] << 16 | e["mean"] << 24 | e["second"] << 25
+
+    def pad(lines):
+        longest = max(len(line) for line in lines)
+        return [line + [(0, 0)] * (longest - len(line)) for line in lines], [len(line) for line in lines]
+
+    places, slots, sends, second, third, ag_sent, rs_sent = [(k, c) for k in range(n) for c in range(cores)], [], [], [], [], [], []
+    for k, c in places:
+        held = {(row, col): a + count * twin for a, twin, row, col, *_ in own[k, c]}
+        slots.append([
+            held.get((row, col), 3 * count + row * half + col) for row in range(per) for col in range(half)
+        ])
+        sends.append([
+            (word(a, k, (twin, up, down, side)), ag_sem(a, twin)) for a, twin, _, _, up, down, side in own[k, c]
+            if up or down or side
+        ])
+        second.append([
+            (word(e["a"], k, [
+                e[f] for f in ("wait", "second", "fup", "fdn", "merge", "cup", "cdn", "comp", "run", "blend")
+            ]), gather_sems(e))
+            for e in gather[k, c]
+        ])
+        third.append([
+            (word(e["a"], k, [
+                e[f] for f in ("comp", "first", "wait", "v", "up", "dn", "fini", "finj", "blend", "side")
+            ]), scatter_sems(e))
+            for e in scatter[k, c]
+        ])
+        ag_sent.append(sum(int(up) + int(down) + int(side) for *_, up, down, side in own[k, c])
+                       + sum(e["fup"] + e["fdn"] + e["cup"] + e["cdn"] for e in gather[k, c]))
+        rs_sent.append(sum(e["up"] + e["dn"] + e["side"] for e in scatter[k, c]))
+    return dict(
+        count=count, slots=slots, sends=pad(sends), gather=pad(second), scatter=pad(third),
+        ag_sent=ag_sent, rs_sent=rs_sent, ag_sems=size_a + size_b, rs_sems=size_u + size_v,
+    )
+
+
+def make_tile_kernel(n, nf, ns, rows, cols, ne, vox_local, n_blocks, regions):
+    per = rows // LANES
+    half = cols // LANES
+    peers = nf * ns
+    plan = plans(n, per, half, ns)
+    count = plan["count"]
+    held = per * half
+
+    def kernel(
+        res, green, active_in, aperture, gain, region_in, strength_in, out,
+        active, region, strength, sem_small,
+        gv, act_col, buf, blocks, rests, img, ar_send, ar_land,
+        wgt, dacc, total, stage, land,
+        sem_g, sem_own, ag_s, ag_r, ar_s, ar_r, rs_s, rs_r,
+    ):
+        z = lax.axis_index("vox")
+        f = lax.axis_index("freq")
+        s = lax.axis_index("sub")
+        has_up = z < n - 1
+        has_down = z > 0
+        z_up = jnp.minimum(z + 1, n - 1)
+        z_down = jnp.maximum(z - 1, 0)
+
+        def remote(src, dst, send, recv, target):
+            return pltpu.make_async_remote_copy(
+                src_ref=src, dst_ref=dst, send_sem=send, recv_sem=recv,
+                device_id=target, device_id_type=MESH,
+            )
+
+        def above(code):
+            return {"vox": z_up, "sub": (code >> 28) & 1}
+
+        def below(code):
+            return {"vox": z_down, "sub": (code >> 29) & 1}
+
+        def peer(k):
+            df, ds = k // ns, k % ns
+            return {"freq": lax.rem(f + df, nf), "sub": lax.rem(s + ds, ns)}
+
+        partner = {"sub": lax.rem(s + 1, ns)}
+
+        def has(code, bit):
+            return ((code >> (18 + bit)) & 1) == 1
+
+        def lines(t):
+            return pl.ds(pl.multiple_of(t * LANES, LANES), LANES)
+
+        role = z * ns + s
+        is_role = [role == r for r in range(n * ns)]
+
+        def pick(values):
+            usual = max(set(values), key=values.count)
+            out_value = jnp.int32(usual)
+            for r, value in enumerate(values):
+                if value != usual:
+                    out_value = jnp.where(is_role[r], jnp.int32(value), out_value)
+            return out_value
+
+        def table(lines):
+            words, lengths = lines
+            columns = [
+                [pick([line[e][part] for line in words]) for e in range(len(words[0]))] for part in (0, 1)
+            ]
+
+            def at(e):
+                found = []
+                for level in columns:
+                    bit = 0
+                    while len(level) > 1:
+                        odd = ((e >> bit) & 1) == 1
+                        paired = [jnp.where(odd, b, a) for a, b in zip(level[::2], level[1::2])]
+                        level, bit = paired + level[len(level) & ~1:], bit + 1
+                    found.append(level[0])
+                return found
+
+            return at, pick(lengths)
+
+        def drain(sem, sent):
+            mine = pick(sent)
+            for m in sorted(set(sent)):
+                @pl.when(mine == m)
+                def _(m=m):
+                    block = buf.at[pl.ds(0, m)]
+                    remote(block, block, sem, ag_r.at[0], {"vox": z_up}).wait_send()
+
+        barrier = pltpu.get_barrier_semaphore()
+        for k in range(1, peers):
+            pl.semaphore_signal(barrier, inc=1, device_id=peer(k), device_id_type=MESH)
+        for c in range(ns):
+            @pl.when(has_up)
+            def _():
+                pl.semaphore_signal(barrier, inc=1, device_id={"vox": z_up, "sub": c}, device_id_type=MESH)
+
+            @pl.when(has_down)
+            def _():
+                pl.semaphore_signal(barrier, inc=1, device_id={"vox": z_down, "sub": c}, device_id_type=MESH)
+
+        green_copy = pltpu.make_async_copy(green, gv, sem_g)
+        small = [
+            pltpu.make_async_copy(a, b, sem_small.at[i])
+            for i, (a, b) in enumerate((
+                (active_in, active), (region_in, region), (strength_in, strength),
+            ))
+        ]
+        for t in range(held):
+            row, col = t // half * LANES, t % half * LANES
+            pltpu.make_async_copy(
+                res.at[row:row + LANES, col:col + LANES], buf.at[pick([line[t] for line in plan["slots"]])], sem_own
+            ).start()
+        for c in small:
+            c.start()
+        green_copy.start()
+        own_at, n_own = table(plan["sends"])
+        gather_at, n_gather = table(plan["gather"])
+        scatter_at, n_scatter = table(plan["scatter"])
+        out[...] = jnp.zeros_like(out)
+        img[...] = jnp.zeros_like(img)
+        blocks[...] = jnp.zeros_like(blocks)
+        rests[...] = jnp.zeros_like(rests)
+        pl.semaphore_wait(barrier, peers - 1 + ns * has_up.astype(jnp.int32) + ns * has_down.astype(jnp.int32))
+
+        pltpu.make_async_copy(buf.at[pl.ds(0, held)], buf.at[pl.ds(held, held)], sem_own).wait()
+
+        def ag_send(source, target, sem, side):
+            remote(buf.at[source], buf.at[target], ag_s, ag_r.at[sem], side).start()
+
+        @pl.loop(0, n_own)
+        def _(e):
+            code, sem = own_at(e)
+            slot = (code & 255) + count * ((code >> 18) & 1)
+
+            @pl.when(has(code, 1))
+            def _():
+                ag_send(slot, slot, sem, above(code))
+
+            @pl.when(has(code, 2))
+            def _():
+                ag_send(slot, slot, sem, below(code))
+
+            @pl.when(has(code, 3))
+            def _():
+                ag_send(slot, slot, sem, partner)
+
+        for c in small:
+            c.wait()
+        for i in range(ne // LANES):
+            line = active[0:1, i * LANES:(i + 1) * LANES].astype(jnp.float32)
+            act_col[i * LANES:(i + 1) * LANES, :] = jnp.broadcast_to(line, (LANES, LANES)).T
+
+        def pair_mask(row_tile, col_tile):
+            rr = lax.broadcasted_iota(jnp.int32, (LANES, LANES), 0) + row_tile * LANES
+            cc = lax.broadcasted_iota(jnp.int32, (LANES, LANES), 1) + col_tile * LANES
+            in_band = jnp.abs(rr - cc) <= aperture[0]
+            row_on = act_col[lines(row_tile), :] > 0.5
+            col_on = active[0:1, lines(col_tile)] > 0
+            return in_band & row_on & col_on
+
+        def block_of(p, q):
+            return lax.div(p, per) * n + lax.div(q, per)
+
+        def inside(p, q):
+            return lines(lax.rem(p, per)), lines(lax.rem(q, per))
+
+        def block_rows(p):
+            return pl.ds(pl.multiple_of(lax.div(p, per) * rows, rows), rows)
+
+        def place(p, q):
+            value = jnp.where(pair_mask(p, q), total[...], 0.0)
+            high = value.astype(jnp.bfloat16)
+            rr, cc = inside(p, q)
+            blocks[block_of(p, q), rr, cc] = high
+            rests[block_of(p, q), rr, cc] = (value - high.astype(jnp.float32)).astype(jnp.bfloat16)
+
+        def image_part(p, q, rest):
+            for v in range(vox_local // CHUNK):
+                vs = pl.ds(v * CHUNK, CHUNK)
+                g = gv[block_rows(q), vs]
+                y = jnp.dot(blocks[block_of(p, q)], g, preferred_element_type=jnp.float32)
+                if rest:
+                    y = y + jnp.dot(rests[block_of(p, q)], g, preferred_element_type=jnp.float32)
+                y = y * gv[block_rows(p), vs].astype(jnp.float32)
+                img[:, vs] += jnp.sum(y.reshape(rows // 8, 8, CHUNK), axis=0)
+
+        green_copy.wait()
+        shape = (LANES, LANES)
+        side_of = lax.broadcasted_iota(jnp.int32, shape, 0) - lax.broadcasted_iota(jnp.int32, shape, 1)
+
+        @pl.loop(0, n_gather)
+        def _(e):
+            code, sems = gather_at(e)
+            a, p, q = code & 255, (code >> 8) & 31, (code >> 13) & 31
+            slot = a + count * ((code >> 19) & 1)
+            merged = a + 2 * count
+            other = (sems >> 16) & 255
+            lower = (sems >> 24) & 1
+            lift = (sems >> 26) & 1
+            landed = jnp.where(lift == 1, other, slot)
+            sem = (sems >> 8) & 255
+
+            @pl.when(has(code, 0))
+            def _():
+                remote(buf.at[landed], buf.at[landed], ag_s, ag_r.at[sems & 255], above(code)).wait_recv()
+
+            @pl.when(lift == 1)
+            def _():
+                both = buf[other].astype(jnp.float32)
+                pairs = jnp.where(side_of == 0, both, both + both.T)
+                away = side_of * (1 - 2 * lower) > 0
+                buf[slot] = jnp.where(away, buf[slot].astype(jnp.float32), pairs).astype(jnp.bfloat16)
+
+            @pl.when(((sems >> 25) & 1) == 1)
+            def _():
+                kept = side_of * (1 - 2 * lower) <= 0
+                buf[a] = jnp.where(kept, buf[other + count * lower].astype(jnp.float32), 0.0).astype(jnp.bfloat16)
+
+            @pl.when(has(code, 2))
+            def _():
+                ag_send(slot, slot, sem, above(code))
+
+            @pl.when(has(code, 3))
+            def _():
+                ag_send(slot, slot, sem, below(code))
+
+            @pl.when(has(code, 4))
+            def _():
+                one = buf[a].astype(jnp.float32)
+                two = buf[a + count].astype(jnp.float32).T
+                passing = (side_of <= 0) & has(code, 9)
+                from_two = side_of * 0 + lower > 0
+                both = jnp.where(passing, jnp.where(from_two, two, one), one + two)
+                buf[merged] = both.astype(jnp.bfloat16)
+                total[...] = both
+
+                @pl.when(has(code, 5))
+                def _():
+                    ag_send(merged, a, sem, above(code))
+
+                @pl.when(has(code, 6))
+                def _():
+                    ag_send(merged, a, sem, below(code))
+
+            @pl.when(has(code, 7))
+            def _():
+                @pl.when(jnp.logical_not(has(code, 4)))
+                def _():
+                    total[...] = buf[a].astype(jnp.float32)
+                place(p, q)
+
+            exact = ((sems >> 27) & 1) == 1
+
+            @pl.when(has(code, 8) & exact)
+            def _():
+                image_part(p, q, True)
+
+            @pl.when(has(code, 8) & jnp.logical_not(exact))
+            def _():
+                image_part(p, q, False)
+
+        for b in range(n_blocks):
+            ar_send[b:b + 1, :] = jnp.sum(img[:, b * BLOCK:(b + 1) * BLOCK], axis=0, keepdims=True)
+        exchanges = [
+            remote(ar_send, ar_land.at[k], ar_s.at[k - 1], ar_r.at[k - 1], peer(k)) for k in range(1, peers)
+        ]
+        for e in exchanges:
+            e.start()
+        strength_map = jnp.concatenate(
+            [jnp.full((1, BLOCK), strength[region[b]], jnp.float32) for b in range(n_blocks)], axis=0
+        )
+
+        drain(ag_s, plan["ag_sent"])
+        for e in exchanges:
+            e.wait_recv()
+        image = ar_send[...]
+        for k in range(1, peers):
+            image = image + ar_land[k]
+        scaled = penalize(image, strength_map)
+        for b in range(n_blocks):
+            img[0:1, b * BLOCK:(b + 1) * BLOCK] = scaled[b:b + 1, :]
+
+        lane_of = lax.broadcasted_iota(jnp.int32, (8, LANES), 1)
+        in_head = (lax.broadcasted_iota(jnp.int32, (8, LANES), 0) == 0) & (lane_of < 8)
+        head_lane = lax.broadcasted_iota(jnp.int32, (1, LANES), 1)
+
+        def encode(value, power=None):
+            if power is None:
+                largest = jnp.max(jnp.max(jnp.abs(value), axis=0, keepdims=True), axis=1, keepdims=True)
+                power = jnp.floor(jnp.log(jnp.maximum(largest, 1e-36)) * (1 / LN2)) + 1.0
+            scaled = value * (STEPS * jnp.exp(power * -LN2))
+            code = (scaled + jnp.where(scaled >= 0, 0.5, -0.5)).astype(jnp.int32)
+            bits = jnp.broadcast_to((power + 128.0).astype(jnp.int32), (8, LANES))
+            head = (code[0:8, :] & -2) | ((bits >> jnp.minimum(lane_of, 8)) & 1)
+            head = jnp.where(in_head, head, code[0:8, :])
+            return jnp.concatenate([head, code[8:, :]], axis=0).astype(jnp.int16)
+
+        def decode(slot):
+            code = land[slot].astype(jnp.int32)
+            bits = jnp.where(head_lane < 8, (code[0:1, :] & 1) << jnp.minimum(head_lane, 8), 0)
+            power = jnp.sum(bits.astype(jnp.float32), axis=1, keepdims=True) - 128.0
+            return code.astype(jnp.float32) * (jnp.exp(power * LN2) * (1 / STEPS)), power
+
+        def scatter(slot, sem, target):
+            return remote(stage.at[slot], land.at[slot], rs_s, rs_r.at[sem], target)
+
+        @pl.loop(0, n_scatter)
+        def _(e):
+            code, sems = scatter_at(e)
+            a, p, q = code & 255, (code >> 8) & 31, (code >> 13) & 31
+            turned = (code >> 21) & 1
+            slot = a + count * turned
+            other = (sems >> 16) & 255
+            wait_sem = sems & 255
+            sem = (sems >> 8) & 255
+
+            block = block_of(p, q)
+            rr, cc = inside(p, q)
+
+            def weigh(part):
+                wgt[part, :] = (gv[part, :].astype(jnp.float32) * img[0:1, :]).astype(jnp.bfloat16)
+
+            @pl.when(has(code, 1))
+            def _():
+                weigh(block_rows(q))
+
+            @pl.when(((sems >> 25) & 1) == 1)
+            def _():
+                weigh(block_rows(p))
+
+            def product(left, right):
+                return lax.dot_general(left, right, (((1,), (1,)), ((), ())), preferred_element_type=jnp.float32)
+
+            @pl.when(has(code, 0))
+            def _():
+                dacc[block] = product(gv[block_rows(p), :], wgt[block_rows(q), :])
+
+            @pl.when(((sems >> 24) & 1) == 1)
+            def _():
+                dacc[block] = 0.5 * (dacc[block] + product(wgt[block_rows(p), :], gv[block_rows(q), :]))
+
+            @pl.when(has(code, 2))
+            def _():
+                scatter(slot, wait_sem, above(code)).wait_recv()
+
+            @pl.when(has(code, 4) | has(code, 5))
+            def _():
+                total[...] = dacc[block, rr, cc]
+
+                @pl.when(has(code, 8))
+                def _():
+                    d = jnp.where(has(code, 4), q, p)
+                    dr, dc = inside(d, d)
+                    total[...] = jnp.where(side_of > 0, total[...], dacc[block_of(d, d), dr, dc])
+
+                @pl.when(has(code, 2))
+                def _():
+                    total[...] += decode(slot)[0]
+
+                stage[slot] = encode(total[...])
+
+            @pl.when(has(code, 4))
+            def _():
+                scatter(slot, sem, above(code)).start()
+
+            @pl.when(has(code, 5))
+            def _():
+                scatter(slot, sem, below(code)).start()
+
+            @pl.when(has(code, 9))
+            def _():
+                both, power = decode(slot)
+                mirrored = jnp.where(side_of <= 0, both, both.T)
+                aside = other + count * turned
+                stage[aside] = encode(mirrored, power)
+                scatter(aside, sem, partner).start()
+
+            @pl.when(has(code, 6) | has(code, 7))
+            def _():
+                total[...] = dacc[block, rr, cc]
+
+                @pl.when(has_down)
+                def _():
+                    total[...] += decode(a)[0]
+
+                @pl.when(has_up)
+                def _():
+                    total[...] += decode(a + count)[0]
+
+            @pl.when(has(code, 6))
+            def _():
+                new = buf[a].astype(jnp.float32) - gain[0] * total[...]
+                out[lines(lax.rem(p, per)), lines(lax.rem(q, half))] = jnp.where(pair_mask(p, q), new, 0.0)
+
+            @pl.when(has(code, 7))
+            def _():
+                new = buf[a + count].astype(jnp.float32) - gain[0] * total[...].T
+                out[lines(lax.rem(q, per)), lines(lax.rem(p, half))] = jnp.where(pair_mask(q, p), new, 0.0)
+
+        for e in exchanges:
+            e.wait_send()
+
+        drain(rs_s, plan["rs_sent"])
+
+    dma = pltpu.SemaphoreType.DMA
+    tile16 = lambda m: pltpu.VMEM((m, LANES, LANES), jnp.bfloat16)
+    scratch = [
+        pltpu.VMEM((1, ne), jnp.int32),
+        pltpu.SMEM((n_blocks,), jnp.int32),
+        pltpu.SMEM((regions,), jnp.float32),
+        dma((3,)),
+        pltpu.VMEM((ne, vox_local), jnp.bfloat16),
+        pltpu.VMEM((ne, LANES), jnp.float32),
+        tile16(3 * count + held),
+        pltpu.VMEM((n * n, rows, rows), jnp.bfloat16),
+        pltpu.VMEM((n * n, rows, rows), jnp.bfloat16),
+        pltpu.VMEM((8, vox_local), jnp.float32),
+        pltpu.VMEM((n_blocks, BLOCK), jnp.float32),
+        pltpu.VMEM((peers, n_blocks, BLOCK), jnp.float32),
+        pltpu.VMEM((ne, vox_local), jnp.bfloat16),
+        pltpu.VMEM((n * n, rows, rows), jnp.float32),
+        pltpu.VMEM((LANES, LANES), jnp.float32),
+        pltpu.VMEM((2 * count, LANES, LANES), jnp.int16),
+        pltpu.VMEM((2 * count, LANES, LANES), jnp.int16),
+        dma, dma, dma, dma((plan["ag_sems"],)),
+        dma((peers - 1,)), dma((peers - 1,)),
+        dma, dma((plan["rs_sems"],)),
+    ]
+    return kernel, scratch
 
 
 def make_kernel(n, nf, ns, rows, cols, ne, vox_local, n_blocks, regions):
@@ -391,13 +1222,24 @@
     return kernel, scratch
 
 
+def tiled(sizes, rows, cols, ne, vox_local):
+    n, ns = sizes["vox"], sizes["sub"]
+    return (
+        rows % LANES == 0 and vox_local % CHUNK == 0 and rows * n == ne and cols * ns == ne
+        and n > 1 and ns > 1 and cols % rows == 0 and ne // LANES <= 32
+        and len(tile_pairs(ne // LANES, REACH)) <= 256
+    )
+
+
 def solution(mesh):
     sizes = dict(mesh.shape)
 
     def body(residual, green, active, aperture, step_gain, block_region, strength):
         _, rows, cols = residual.shape
         _, ne, vox_local = green.shape
-        kernel, scratch = make_kernel(
+        tiles = tiled(sizes, rows, cols, ne, vox_local)
+        make = make_tile_kernel if tiles else make_kernel
+        kernel, scratch = make(
             sizes["vox"], sizes["freq"], sizes["sub"], rows, cols, ne, vox_local,
             block_region.shape[0], strength.shape[0],
         )
@@ -406,11 +1248,11 @@
         updated = pl.pallas_call(
             kernel,
             out_shape=jax.ShapeDtypeStruct((rows, cols), jnp.float32),
-            in_specs=[hbm] * 7,
+            in_specs=[hbm] * 3 + [pl.BlockSpec(memory_space=pltpu.SMEM) if tiles else hbm] * 2 + [hbm] * 2,
             out_specs=vmem,
             scratch_shapes=scratch,
             compiler_params=pltpu.CompilerParams(
-                collective_id=0, has_side_effects=True, vmem_limit_bytes=24 * 1024 * 1024
+                collective_id=0, has_side_effects=True, vmem_limit_bytes=32 * 1024 * 1024
             ),
             name="imaging_step",
         )(*[

time: 44.8 us -> 35.6 us (0.79)
  Pallas kernels: 42.5 us -> 33.3 us
    pallas_call x1, Pallas kernels: 42.5 us -> 33.3 us  [body(): pl.pallas_call(kernel, out_shape=jax.ShapeDtypeStruct((rows, cols), jnp.f...]
where the time goes in v2:
time: 35.6 us; the launch traced here: 35.4 us
  Pallas kernels  33.3 us (94%)
  between operations  1.3 us (4%)
  local copies, waits for them, and re-layouts  0.8 us (2%)
    pallas_call x1, Pallas kernels, body(): pl.pallas_call(kernel, out_shape=jax.ShapeDtypeStruct((rows, cols), jnp.f...  33.3 us
    unnamed x1, local copies, waits for them, and re-layouts  0.8 us

profile of v2, /device:TPU:0, one launch (start us, length us, event | category | flops | bytes accessed | tf_op | source)
XLA Modules:
  0.0 35.4 jit_solution(5947340333977799413)
XLA Ops:
  1.3 33.3 %imaging_step.1 = f32[256,512]{1,0:T(8,128)S(1)} custom-call(bf16[256,512]{1,0:T(8,128)(2,1)} %bitcast.5, bf16[1024,2048]{1,0:T(8,128)(2,1)} %bitcast.4, s32[1,1024]{1,0:T(1,128)} %active_in.1, s32[1]{0:T(128)S(6)} %copy.9.aperture, f32[1]{0:T(128)S(6)} %copy.10.gain, s32[16]{0:T(128)} %region_in.1, f32[16]{0:T(128)} %strength_in.1), custom_call_target="tpu_custom_call" | custom-call | tf_op jit(solution)/shard_map/imaging_step/pallas_call | solution.py:1248
  34.6 0.8 %copy.11 = f32[1,256,512]{2,1,0:T(8,128)} copy(f32[1,256,512]{2,1,0:T(8,128)S(1)} %bitcast.3) | data formatting | bytes 1048576

commit v3 on v2

--- a/solution.py
+++ b/solution.py
@@ -432,7 +432,7 @@
         res, green, active_in, aperture, gain, region_in, strength_in, out,
         active, region, strength, sem_small,
         gv, act_col, buf, blocks, rests, img, ar_send, ar_land,
-        wgt, dacc, total, stage, land,
+        wgt, dacc, total, powers, size, stage, land,
         sem_g, sem_own, ag_s, ag_r, ar_s, ar_r, rs_s, rs_r,
     ):
         z = lax.axis_index("vox")
@@ -699,26 +699,28 @@
         for b in range(n_blocks):
             img[0:1, b * BLOCK:(b + 1) * BLOCK] = scaled[b:b + 1, :]
 
-        lane_of = lax.broadcasted_iota(jnp.int32, (8, LANES), 1)
-        in_head = (lax.broadcasted_iota(jnp.int32, (8, LANES), 0) == 0) & (lane_of < 8)
-        head_lane = lax.broadcasted_iota(jnp.int32, (1, LANES), 1)
-
-        def encode(value, power=None):
-            if power is None:
-                largest = jnp.max(jnp.max(jnp.abs(value), axis=0, keepdims=True), axis=1, keepdims=True)
-                power = jnp.floor(jnp.log(jnp.maximum(largest, 1e-36)) * (1 / LN2)) + 1.0
+        head_row = lax.broadcasted_iota(jnp.int32, (8, LANES), 0)
+
+        def power_of(value):
+            largest = jnp.max(jnp.max(jnp.abs(value), axis=0, keepdims=True), axis=1, keepdims=True)
+            power = jnp.floor(jnp.log(jnp.maximum(largest, 1e-36)) * (1 / LN2)) + 1.0
+            return jnp.broadcast_to(power, (8, LANES))
+
+        def encode(value, power):
             scaled = value * (STEPS * jnp.exp(power * -LN2))
             code = (scaled + jnp.where(scaled >= 0, 0.5, -0.5)).astype(jnp.int32)
             bits = jnp.broadcast_to((power + 128.0).astype(jnp.int32), (8, LANES))
-            head = (code[0:8, :] & -2) | ((bits >> jnp.minimum(lane_of, 8)) & 1)
-            head = jnp.where(in_head, head, code[0:8, :])
+            head = (code[0:8, :] & -2) | ((bits >> head_row) & 1)
             return jnp.concatenate([head, code[8:, :]], axis=0).astype(jnp.int16)
 
         def decode(slot):
             code = land[slot].astype(jnp.int32)
-            bits = jnp.where(head_lane < 8, (code[0:1, :] & 1) << jnp.minimum(head_lane, 8), 0)
-            power = jnp.sum(bits.astype(jnp.float32), axis=1, keepdims=True) - 128.0
+            bits = jnp.sum(((code[0:8, :] & 1) << head_row).astype(jnp.float32), axis=0, keepdims=True)
+            power = bits - 128.0
             return code.astype(jnp.float32) * (jnp.exp(power * LN2) * (1 / STEPS)), power
+
+        def sub_tile(p, q):
+            return (block_of(p, q) * per + lax.rem(p, per)) * per + lax.rem(q, per)
 
         def scatter(slot, sem, target):
             return remote(stage.at[slot], land.at[slot], rs_s, rs_r.at[sem], target)
@@ -762,21 +764,33 @@
             def _():
                 scatter(slot, wait_sem, above(code)).wait_recv()
 
+            @pl.when(has(code, 0))
+            def _():
+                for x in range(per * per):
+                    r0, c0 = x // per * LANES, x % per * LANES
+                    powers[block * per * per + x] = power_of(dacc[block, r0:r0 + LANES, c0:c0 + LANES])
+
             @pl.when(has(code, 4) | has(code, 5))
             def _():
                 total[...] = dacc[block, rr, cc]
+                size[...] = powers[sub_tile(p, q)]
 
                 @pl.when(has(code, 8))
                 def _():
                     d = jnp.where(has(code, 4), q, p)
                     dr, dc = inside(d, d)
                     total[...] = jnp.where(side_of > 0, total[...], dacc[block_of(d, d), dr, dc])
+                    size[...] = jnp.maximum(size[...], powers[sub_tile(d, d)])
 
                 @pl.when(has(code, 2))
                 def _():
-                    total[...] += decode(slot)[0]
-
-                stage[slot] = encode(total[...])
+                    value, power = decode(slot)
+                    summed = jnp.maximum(size[0:1, :], power) + 1.0
+                    stage[slot] = encode(total[...] + value, summed)
+
+                @pl.when(jnp.logical_not(has(code, 2)))
+                def _():
+                    stage[slot] = encode(total[...], size[0:1, :])
 
             @pl.when(has(code, 4))
             def _():
@@ -839,6 +853,8 @@
         pltpu.VMEM((ne, vox_local), jnp.bfloat16),
         pltpu.VMEM((n * n, rows, rows), jnp.float32),
         pltpu.VMEM((LANES, LANES), jnp.float32),
+        pltpu.VMEM((n * n * per * per, 8, LANES), jnp.float32),
+        pltpu.VMEM((8, LANES), jnp.float32),
         pltpu.VMEM((2 * count, LANES, LANES), jnp.int16),
         pltpu.VMEM((2 * count, LANES, LANES), jnp.int16),
         dma, dma, dma, dma((plan["ag_sems"],)),

time: 35.6 us -> 34.7 us (0.975)
  Pallas kernels: 33.3 us -> 32.4 us
    pallas_call x1, Pallas kernels: 33.3 us -> 32.4 us  [body(): pl.pallas_call(kernel, out_shape=jax.ShapeDtypeStruct((rows, cols), jnp.f...]
where the time goes in v3:
time: 34.7 us; the launch traced here: 34.5 us
  Pallas kernels  32.4 us (93%)
  between operations  1.3 us (4%)
  local copies, waits for them, and re-layouts  0.8 us (2%)
    pallas_call x1, Pallas kernels, body(): pl.pallas_call(kernel, out_shape=jax.ShapeDtypeStruct((rows, cols), jnp.f...  32.4 us
    unnamed x1, local copies, waits for them, and re-layouts  0.8 us

profile of v3, /device:TPU:0, one launch (start us, length us, event | category | flops | bytes accessed | tf_op | source)
XLA Modules:
  0.0 34.5 jit_solution(7946828847822245714)
XLA Ops:
  1.3 32.4 %imaging_step.1 = f32[256,512]{1,0:T(8,128)S(1)} custom-call(bf16[256,512]{1,0:T(8,128)(2,1)} %bitcast.5, bf16[1024,2048]{1,0:T(8,128)(2,1)} %bitcast.4, s32[1,1024]{1,0:T(1,128)} %active_in.1, s32[1]{0:T(128)S(6)} %copy.9.aperture, f32[1]{0:T(128)S(6)} %copy.10.gain, s32[16]{0:T(128)} %region_in.1, f32[16]{0:T(128)} %strength_in.1), custom_call_target="tpu_custom_call" | custom-call | tf_op jit(solution)/shard_map/imaging_step/pallas_call | solution.py:1264
  33.7 0.8 %copy.11 = f32[1,256,512]{2,1,0:T(8,128)} copy(f32[1,256,512]{2,1,0:T(8,128)S(1)} %bitcast.3) | data formatting | bytes 1048576
